TPU v7x, 32 devices: a whole 2x2x4 slice. The times are simulated.
32 devices in a mesh: section: 2 (over x), fsdp: 16 (over z, y, core).
Axes of the slice: x: 2, y: 2, z: 4, core: 2. Of those that a mesh axis runs over, the one named last changes fastest.
Arguments:
- hidden_in: bfloat16 [16, 128, 4096], P('fsdp', 'section'), may hold values from -40 to 40
- queries: bfloat16 [2, 16, 128, 4096], P('section', 'fsdp'), may hold values from -260 to 260
- key_weight: bfloat16 [2, 4096, 512], P('section', 'fsdp'), may hold values from -0.09375 to 0.09375
- value_weight: bfloat16 [2, 4096, 512], P('section', 'fsdp'), may hold values from -0.09375 to 0.09375
- norm_gain: float32 [2, 4096], P('section'), may hold values from 0.5 to 1.5
Outputs:
- section_outputs: bfloat16 [2, 16, 128, 4096], P('section', 'fsdp')
All inputs are finite; a program needn't handle non-finite values.
Results may differ from a plain program's by a relative error of at most 0.013.
Values may be sent and summed in bfloat16 or wider, within the bound.
A program may use at most 64 MiB of HBM per device.

v0:
```python
import functools
import math

import jax
import jax.numpy as jnp
import numpy as np
from jax import lax
from jax.experimental import pallas as pl
from jax.experimental.pallas import tpu as pltpu
from jax.sharding import PartitionSpec as P

HD = 128
EPS = 1e-05
MESH = pl.DeviceIdType.MESH


def rope_tables(rows):
    half = HD // 2
    frequency = np.exp(np.arange(half, dtype=np.float32) * np.float32(-2.0 * math.log(10000.0) / HD))
    angles = np.arange(rows, dtype=np.float32)[:, None] * frequency[None, :].astype(np.float32)
    cosine, sine = np.cos(angles), np.sin(angles)
    return (
        np.concatenate([cosine, cosine], 1).astype(np.float32),
        np.concatenate([-sine, sine], 1).astype(np.float32),
    )


def rope(u, cosine, sine):
    return u * cosine + pltpu.roll(u, HD // 2, 1) * sine


def kernel(
    n, sections, outer, inner,
    hid, q_in, kw, vw, gain_in, cos_in, sin_in,
    out,
    w, xin, xs, qs, qp, normed, acc, kv, kvp, gain, cos_ref, sin_ref,
    w_recv, w_send, own_sem, hid_recv, hid_send, hid_own, q_sem, kv_sem, x_sem, load_sem,
):
    s = lax.axis_index("section")
    f = lax.axis_index("fsdp")
    core = lax.rem(f, 2)
    chip = f // 2
    i = lax.rem(chip, inner)
    o = chip // inner
    rows, width = xs.shape
    part = hid.shape[1]
    kvw = kw.shape[2]
    kv_heads = kvw // HD
    group = width // kvw
    depth = kw.shape[1]

    def index(oo, ii, cc):
        return (oo * inner + ii) * 2 + cc

    own_k = pltpu.make_async_copy(kw.at[0], w.at[f, 0], own_sem.at[0])
    own_v = pltpu.make_async_copy(vw.at[0], w.at[f, 1], own_sem.at[1])
    own_k.start()
    own_v.start()
    loads = [
        pltpu.make_async_copy(src, dst, load_sem.at[at])
        for at, (src, dst) in enumerate(
            ((q_in.at[0, 0], qs), (gain_in, gain), (cos_in, cos_ref), (sin_in, sin_ref)))
    ]
    for load in loads:
        load.start()

    targets = (
        (o > 0, index(o - 1, i, core)),
        (o < outer - 1, index(o + 1, i, core)),
        (i > 0, index(o, i - 1, core)),
        (i < inner - 1, index(o, i + 1, core)),
        (None, index(o, i, 1 - core)),
    )

    barrier = pltpu.get_barrier_semaphore()
    for cond, target in targets:
        def greet(target=target):
            pl.semaphore_signal(barrier, inc=1, device_id={"fsdp": target}, device_id_type=MESH)
        if cond is None:
            greet()
        else:
            pl.when(cond)(greet)
    for step in range(1, sections):
        pl.semaphore_signal(
            barrier, inc=1, device_id={"section": lax.rem(s + step, sections)}, device_id_type=MESH
        )
    expected = (
        jnp.where(o > 0, 1, 0) + jnp.where(o < outer - 1, 1, 0)
        + jnp.where(i > 0, 1, 0) + jnp.where(i < inner - 1, 1, 0) + sections
    )
    pl.semaphore_wait(barrier, expected)

    few = max(16, depth // 8)
    first = (depth - few + 16) // 32 * 16
    cuts = (pl.ds(0, first), pl.ds(first, depth - few - first), pl.ds(depth - few, few))
    mains, tail = (0, 1), 2

    def w_copy(which, way, origin):
        piece = w.at[origin, :, cuts[which]]
        return pltpu.make_async_remote_copy(
            src_ref=piece, dst_ref=piece,
            send_sem=w_send.at[which, way, origin], recv_sem=w_recv.at[which, origin],
            device_id={"fsdp": targets[way][1]}, device_id_type=MESH,
        )

    def w_start(which, way, origin):
        cond = targets[way][0]
        if cond is None:
            w_copy(which, way, origin).start()
        else:
            pl.when(cond)(lambda: w_copy(which, way, origin).start())

    own_k.wait()
    own_v.wait()
    for way in (2, 3):
        w_start(tail, way, f)
    for which in mains:
        for way in range(5):
            w_start(which, way, f)
    for way in (0, 1, 4):
        w_start(tail, way, f)

    mine = pl.ds(pl.multiple_of(s * part, part), part)

    def hid_copy(to):
        dst = xs if to == 0 else xin
        return pltpu.make_async_remote_copy(
            src_ref=hid.at[0], dst_ref=dst.at[mine], send_sem=hid_send.at[to],
            recv_sem=hid_recv.at[s], device_id={"section": to}, device_id_type=MESH,
        )

    def hid_local(to):
        dst = xs if to == 0 else xin
        return pltpu.make_async_copy(hid.at[0], dst.at[mine], hid_own)

    for to in range(min(2, sections)):
        pl.when(s != to)(lambda to=to: hid_copy(to).start())
        pl.when(s == to)(lambda to=to: hid_local(to).start())

    q_copy = pltpu.make_async_remote_copy(
        src_ref=q_in.at[0, 0], dst_ref=qp, send_sem=q_sem.at[0], recv_sem=q_sem.at[1],
        device_id={"section": jnp.minimum(s + 1, sections - 1)}, device_id_type=MESH,
    )
    def kv_copy(g):
        return pltpu.make_async_remote_copy(
            src_ref=kv.at[g], dst_ref=kvp.at[g], send_sem=kv_sem.at[0, g], recv_sem=kv_sem.at[1, g],
            device_id={"section": jnp.minimum(s + 1, sections - 1)}, device_id_type=MESH,
        )

    x_copy = pltpu.make_async_remote_copy(
        src_ref=xs, dst_ref=xin, send_sem=x_sem.at[0], recv_sem=x_sem.at[1],
        device_id={"section": jnp.minimum(s + 1, sections - 1)}, device_id_type=MESH,
    )
    last = s == sections - 1
    pl.when(jnp.logical_not(last))(lambda: q_copy.start())

    for load in loads:
        load.wait()

    def rope_queries(ref):
        def one(h, _):
            cols = pl.ds(pl.multiple_of(h * HD, HD), HD)
            u = ref[:, cols].astype(jnp.float32)
            ref[:, cols] = rope(u, cos_ref[...], sin_ref[...]).astype(jnp.bfloat16)
            return 0
        lax.fori_loop(0, width // HD, one, 0)

    rope_queries(qs)

    def hid_arrive(to):
        hid_local(to).wait()
        dst = xs if to == 0 else xin
        for step in range(1, sections):
            j = lax.rem(to + step, sections)
            pltpu.make_async_remote_copy(
                src_ref=hid.at[0], dst_ref=dst.at[pl.ds(j * part, part)],
                send_sem=hid_send.at[to], recv_sem=hid_recv.at[j],
                device_id={"section": to}, device_id_type=MESH,
            ).wait_recv()

    block = 16

    def norm():
        def one(r, _):
            at = pl.ds(pl.multiple_of(r * block, block), block)
            x = xs[at, :].astype(jnp.float32)
            mean_square = jnp.mean(x * x, axis=-1, keepdims=True)
            y = (x * lax.rsqrt(mean_square + EPS) * gain[...]).astype(jnp.bfloat16)
            for pair in range(n // 2):
                normed[pair, at, :] = y[:, pair * 2 * depth:(pair + 1) * 2 * depth]
            return 0
        lax.fori_loop(0, rows // block, one, 0)

    def project(pair):
        a = normed[pair]
        for half in range(2):
            b = w[pl.ds(pair * 2, 2), half].reshape(2 * depth, kvw)
            acc[half] += jnp.dot(a, b, preferred_element_type=jnp.float32)

    acc[...] = jnp.zeros_like(acc)

    def arrive(which, origin, ways):
        w_copy(which, 4, origin).wait_recv()
        for way in ways:
            w_start(which, way, origin)

    def relay(which, origin, ways):
        arrive(which, origin, ways)

    def from_other(which, origin, ways):
        arrive(which, origin, ())

    def project_pair(which, origin, ways):
        if which == tail - 1:
            project(origin // 2)

    def sides(t, act):
        for sign, way in ((-1, 1), (1, 0)):
            far = o - t if sign < 0 else o + t
            there = (far >= 0) if sign < 0 else ((far < outer) & (t > 0))
            act(far, there, way)

    def around(there, act):
        for d in range(1, inner):
            pl.when(there & (i - d >= 0))(lambda d=d: act(i - d, 3))
            pl.when(there & (i + d < inner))(lambda d=d: act(i + d, 2))

    def along_outer(t, c, receive):
        for which in mains:
            def act(far, there, way, which=which):
                pl.when(there)(lambda: receive(which, index(far, i, c), (way, 2, 3, 4)))
            sides(t, act)

        def act_tail(far, there, way):
            pl.when(there)(lambda: receive(tail, index(far, i, c), (way, 4)))
            around(there, lambda ii, _: receive(tail, index(far, ii, c), (way, 4)))
        sides(t, act_tail)

    def along_inner(t, c, receive):
        for which in mains:
            def act(far, there, _, which=which):
                around(there, lambda ii, way: receive(which, index(far, ii, c), (way, 4)))
            sides(t, act)

    def first_inner(c, receive):
        around(o >= 0, lambda ii, way: receive(tail, index(o, ii, c), (way, 0, 1, 4)))

    first_inner(core, relay)

    def step(t, _):
        along_outer(t + 1, core, relay)

        @pl.when((t == 0) & (s == 0))
        def _():
            hid_arrive(0)
            norm()

        @pl.when(t == 0)
        def _():
            for which in (*mains, tail):
                arrive(which, index(o, i, 1 - core), ())
            first_inner(1 - core, from_other)

        along_inner(t, core, relay)
        along_outer(t + 1, 1 - core, from_other)
        along_inner(t, 1 - core, from_other)

        @pl.when(s == 0)
        def _():
            pl.when(t == 0)(lambda: project(chip))
            along_outer(t + 1, core, project_pair)
            along_inner(t, core, project_pair)

        return 0

    lax.fori_loop(0, outer, step, 0)

    row = lax.broadcasted_iota(jnp.int32, (rows, rows), 0)
    col = lax.broadcasted_iota(jnp.int32, (rows, rows), 1)
    scale = math.log2(math.e) / math.sqrt(HD)

    def attend(q_ref, kv_ref, x_ref, o_write, ready):
        ones = jnp.ones((rows, HD), jnp.bfloat16)
        allowed = (col <= row)[None]

        def one(g, _):
            ready(g)
            k = kv_ref[g, 0]
            v = jnp.concatenate([kv_ref[g, 1], ones], axis=1)
            base = g * group * HD
            cols = [pl.ds(pl.multiple_of(base + h * HD, HD), HD) for h in range(group)]
            q = jnp.concatenate([q_ref[:, c] for c in cols], axis=0)
            scores = lax.dot_general(q, k, (((1,), (1,)), ((), ())), preferred_element_type=jnp.float32)
            scores = jnp.where(allowed, scores.reshape(group, rows, rows), -1e30)
            top = jnp.max(scores, axis=-1, keepdims=True)
            p = jnp.exp2((scores - top) * scale).astype(jnp.bfloat16).reshape(group * rows, rows)
            mixed = jnp.dot(p, v, preferred_element_type=jnp.float32)
            mixed = mixed[:, :HD] / mixed[:, HD:]
            for h in range(group):
                o_write(cols[h], (
                    x_ref[:, cols[h]].astype(jnp.float32) + mixed[h * rows:(h + 1) * rows]
                ).astype(jnp.bfloat16))
            return 0

        lax.fori_loop(0, kv_heads, one, 0)

    def write_xs(c, value):
        xs[:, c] = value

    def write_out(c, value):
        out[0, 0, :, c] = value

    @pl.when(s > 0)
    def _():
        q_copy.wait_recv()
        rope_queries(qp)
        pl.when(s == 1)(lambda: hid_arrive(1))
        if sections > 2:
            pl.when(s > 1)(lambda: x_copy.wait_recv())
        attend(qp, kvp, xin, write_xs, lambda g: kv_copy(g).wait_recv())
        if sections > 2:
            pl.when(jnp.logical_not(last))(lambda: x_copy.start())
        norm()
        def one(j, _):
            project(j)
            return 0
        lax.fori_loop(0, n // 2, one, 0)

    for h in range(kv_heads):
        at = slice(h * HD, (h + 1) * HD)
        kv[h, 0] = rope(acc[0, :, at], cos_ref[...], sin_ref[...]).astype(jnp.bfloat16)
        kv[h, 1] = acc[1, :, at].astype(jnp.bfloat16)
        pl.when(jnp.logical_not(last))(lambda h=h: kv_copy(h).start())
    attend(qs, kv, xs, write_out, lambda g: None)

    def drain(which, origin, ways):
        for way in ways:
            cond = targets[way][0]
            if cond is None:
                w_copy(which, way, origin).wait_send()
            else:
                pl.when(cond)(lambda way=way: w_copy(which, way, origin).wait_send())

    for which in (*mains, tail):
        drain(which, f, range(5))
    first_inner(core, drain)

    def drain_step(t, _):
        along_outer(t + 1, core, drain)
        along_inner(t, core, drain)
        return 0

    lax.fori_loop(0, outer, drain_step, 0)
    for to in range(min(2, sections)):
        pl.when(s != to)(lambda to=to: hid_copy(to).wait_send())

    @pl.when(jnp.logical_not(last))
    def _():
        q_copy.wait_send()
        for h in range(kv_heads):
            kv_copy(h).wait_send()
        if sections > 2:
            pl.when(s > 0)(lambda: x_copy.wait_send())


def solution(mesh):
    sections, n = mesh.shape["section"], mesh.shape["fsdp"]
    chips = n // 2
    outer = 4 if chips % 4 == 0 else 1
    inner = chips // outer

    def body(hidden_in, queries, key_weight, value_weight, norm_gain):
        rows, width = queries.shape[2:]
        depth, kvw = key_weight.shape[1:]
        cosine, sine = rope_tables(rows)
        hbm = pl.BlockSpec(memory_space=pltpu.HBM)
        vmem = pl.BlockSpec(memory_space=pltpu.VMEM)
        dma = pltpu.SemaphoreType.DMA
        bf16, f32 = jnp.bfloat16, jnp.float32
        return pl.pallas_call(
            functools.partial(kernel, n, sections, outer, inner),
            out_shape=jax.ShapeDtypeStruct(queries.shape, bf16),
            in_specs=[hbm] * 7,
            out_specs=vmem,
            scratch_shapes=[
                pltpu.VMEM((n, 2, depth, kvw), bf16),
                pltpu.VMEM((rows, width), bf16),
                pltpu.VMEM((rows, width), bf16),
                pltpu.VMEM((rows, width), bf16),
                pltpu.VMEM((rows, width), bf16),
                pltpu.VMEM((n // 2, rows, 2 * depth), bf16),
                pltpu.VMEM((2, rows, kvw), f32),
                pltpu.VMEM((kvw // HD, 2, rows, HD), bf16),
                pltpu.VMEM((kvw // HD, 2, rows, HD), bf16),
                pltpu.VMEM((1, width), f32),
                pltpu.VMEM((rows, HD), f32),
                pltpu.VMEM((rows, HD), f32),
                dma((3, n)), dma((3, 5, n)), dma((2,)), dma((sections,)), dma((2,)), dma,
                dma((2,)), dma((2, kvw // HD)), dma((2,)), dma((4,)),
            ],
            compiler_params=pltpu.CompilerParams(
                collective_id=0, has_side_effects=True, vmem_limit_bytes=28 * 2**20
            ),
        )(*(
            pltpu.with_memory_space_constraint(x, pltpu.HBM)
            for x in (hidden_in, queries, key_weight, value_weight, norm_gain, jnp.asarray(cosine), jnp.asarray(sine))
        ))

    placed = (
        P("fsdp", "section", None),
        P("section", "fsdp", None, None),
        P("section", "fsdp", None),
        P("section", "fsdp", None),
        P("section", None),
    )
    return jax.shard_map(
        body, mesh=mesh, in_specs=placed, out_specs=P("section", "fsdp", None, None), check_vma=False
    )
```

profile of v0, /device:TPU:3, one launch (start us, length us, event | category | flops | bytes accessed | tf_op | source)
XLA Modules:
  0.0 64.9 jit_solution(1056515498181626641)
XLA Ops:
  0.0 63.9 %shard_map.73 = bf16[1,1,128,4096]{3,2,1,0:T(8,128)(2,1)S(1)} custom-call(bf16[1,64,4096]{2,1,0:T(8,128)(2,1)} %hid.1, bf16[1,1,128,4096]{3,2,1,0:T(8,128)(2,1)} %q_in.1, bf16[1,256,512]{2,1,0:T(8,128)(2,1)} %kw.1, bf16[1,256,512]{2,1,0:T(8,128)(2,1)} %vw.1, f32[1,4096]{1,0:T(1,128)} %gain_in.1, f32[128,128]{1,0:T(8,128)} %constant.4.clone.cos_in, ...), custom_call_target="tpu_custom_call" | custom-call | tf_op jit(solution)/shard_map/pallas_call | solution.py:380
  64.0 1.0 %copy.9 = bf16[1,1,128,4096]{3,2,1,0:T(8,128)(2,1)} copy(bf16[1,1,128,4096]{3,2,1,0:T(8,128)(2,1)S(1)} %shard_map.73) | data formatting | bytes 2097152
where the time goes:
time: 65.1 us; the launch traced here: 64.9 us
  Pallas kernels  63.9 us (98%)
  local copies, waits for them, and re-layouts  0.97 us (1%)
    pallas_call x1, Pallas kernels, body(): pl.pallas_call(functools.partial(kernel, n, sections, outer, inner), out_...  63.9 us

commit v1 on v0

v1 whole, which is shorter than its diff:
```python
import functools
import math

import jax
import jax.numpy as jnp
import numpy as np
from jax import lax
from jax.experimental import pallas as pl
from jax.experimental.pallas import tpu as pltpu
from jax.sharding import PartitionSpec as P

HD = 128
EPS = 1e-05
MESH = pl.DeviceIdType.MESH


def rope_tables(rows):
    half = HD // 2
    frequency = np.exp(np.arange(half, dtype=np.float32) * np.float32(-2.0 * math.log(10000.0) / HD))
    angles = np.arange(rows, dtype=np.float32)[:, None] * frequency[None, :].astype(np.float32)
    cosine, sine = np.cos(angles), np.sin(angles)
    return (
        np.concatenate([cosine, cosine], 1).astype(np.float32),
        np.concatenate([-sine, sine], 1).astype(np.float32),
    )


def rope(u, cosine, sine):
    return u * cosine + pltpu.roll(u, HD // 2, 1) * sine


def kernel(
    n, sections, outer, inner,
    hid, q_in, kw, vw, gain_in, cos_in, sin_in,
    out,
    w, stage, xs, x1, xg, q0, q1, acc, kv0, kv1, gains, ssq, cos_ref, sin_ref,
    w_recv, w_send, stage_send, own_sem, load_sem, gain_sem, hid_recv, hid_send, hid_own,
    q_sem, x1_sem, kv_sem, pass_sem,
):
    s = lax.axis_index("section")
    f = lax.axis_index("fsdp")
    side = lax.rem(s, 2)
    pair = s // 2
    mate = {"section": s + 1 - 2 * side}
    core = lax.rem(f, 2)
    chip = f // 2
    i = lax.rem(chip, inner)
    o = chip // inner
    rows, width = xs.shape
    part = hid.shape[1]
    kvw = kw.shape[2]
    kv_heads = kvw // HD
    mine_heads = kv_heads // 2
    slots = 2 * mine_heads
    group = width // kvw
    gw = group * HD
    depth = kw.shape[1]
    chips = n // 2
    blk = width // chips
    half = width // 2
    pieces = half // blk

    def index(oo, ii, cc):
        return (oo * inner + ii) * 2 + cc

    local = []
    for hh in range(mine_heads):
        for to_mate in (False, True):
            head = (1 - side if to_mate else side) * mine_heads + hh
            cols = pl.ds(pl.multiple_of(head * HD, HD), HD)
            for kind, src in enumerate((kw, vw)):
                lanes = pl.ds(kind * HD, HD)
                dst = stage.at[hh, :, lanes] if to_mate else w.at[side * mine_heads + hh, f, :, lanes]
                local.append(pltpu.make_async_copy(src.at[0, :, cols], dst, own_sem.at[len(local)]))
    for copy in local:
        copy.start()
    loads = [
        pltpu.make_async_copy(src, dst, load_sem.at[at])
        for at, (src, dst) in enumerate(
            ((gain_in, gains.at[side]), (cos_in, cos_ref), (sin_in, sin_ref)))
    ]
    for load in loads:
        load.start()

    my_q = pl.ds(pl.multiple_of(side * half, half), half)

    def q_local(which):
        if which == 0:
            return pltpu.make_async_copy(q_in.at[0, 0, :, pl.ds(0, half)], q0, load_sem.at[3])
        return pltpu.make_async_copy(q_in.at[0, 0], q1, load_sem.at[3])

    pl.when(side == 0)(lambda: q_local(0).start())
    pl.when(side == 1)(lambda: q_local(1).start())

    targets = (
        (o > 0, index(o - 1, i, core)),
        (o < outer - 1, index(o + 1, i, core)),
        (i > 0, index(o, i - 1, core)),
        (i < inner - 1, index(o, i + 1, core)),
        (None, index(o, i, 1 - core)),
    )

    barrier = pltpu.get_barrier_semaphore()
    for cond, target in targets:
        def greet(target=target):
            pl.semaphore_signal(barrier, inc=1, device_id={"fsdp": target}, device_id_type=MESH)
        if cond is None:
            greet()
        else:
            pl.when(cond)(greet)
    for step in range(1, sections):
        pl.semaphore_signal(
            barrier, inc=1, device_id={"section": lax.rem(s + step, sections)}, device_id_type=MESH
        )
    expected = (
        jnp.where(o > 0, 1, 0) + jnp.where(o < outer - 1, 1, 0)
        + jnp.where(i > 0, 1, 0) + jnp.where(i < inner - 1, 1, 0) + sections
    )
    pl.semaphore_wait(barrier, expected)

    few = max(16, (depth * 3 // 16 + 8) // 16 * 16)
    cuts = (pl.ds(0, depth - few), pl.ds(depth - few, few))
    main, tail = 0, 1

    def w_copy(k, which, way, origin):
        piece = w.at[k, origin, cuts[which]]
        return pltpu.make_async_remote_copy(
            src_ref=piece, dst_ref=piece,
            send_sem=w_send.at[k, which, way, origin // 2], recv_sem=w_recv.at[k, which, origin],
            device_id={"fsdp": targets[way][1]}, device_id_type=MESH,
        )

    def on_way(way, act):
        cond = targets[way][0]
        if cond is None:
            act()
        else:
            pl.when(cond)(act)

    def w_start(k, which, way, origin):
        on_way(way, lambda: w_copy(k, which, way, origin).start())

    def stage_copy(layer, hh, which):
        k = layer * mine_heads + hh
        return pltpu.make_async_remote_copy(
            src_ref=stage.at[hh, cuts[which]], dst_ref=w.at[k, f, cuts[which]],
            send_sem=stage_send.at[hh, which], recv_sem=w_recv.at[k, which, f],
            device_id=mate, device_id_type=MESH,
        )

    def send_stage(hh):
        for which in (tail, main):
            stage_copy(side, hh, which).start()

    gain_copy = pltpu.make_async_remote_copy(
        src_ref=gain_in, dst_ref=gains.at[side], send_sem=gain_sem.at[0], recv_sem=gain_sem.at[1],
        device_id=mate, device_id_type=MESH,
    )
    gain_back = pltpu.make_async_remote_copy(
        src_ref=gain_in, dst_ref=gains.at[1 - side], send_sem=gain_sem.at[0], recv_sem=gain_sem.at[1],
        device_id=mate, device_id_type=MESH,
    )

    tokens = pl.ds(pl.multiple_of(s * part, part), part)

    def hid_copy(to):
        return pltpu.make_async_remote_copy(
            src_ref=hid.at[0], dst_ref=xs.at[tokens], send_sem=hid_send.at[to],
            recv_sem=hid_recv.at[s], device_id={"section": to}, device_id_type=MESH,
        )

    hid_local = pltpu.make_async_copy(hid.at[0], xs.at[tokens], hid_own)

    def send_hidden():
        for to in range(2):
            pl.when(s != to)(lambda to=to: hid_copy(to).start())
        pl.when(s < 2)(lambda: hid_local.start())

    def q_copy(g):
        return pltpu.make_async_remote_copy(
            src_ref=q_in.at[0, 0, :, pl.ds(half + g * gw, gw)], dst_ref=q0.at[:, pl.ds(g * gw, gw)],
            send_sem=q_sem.at[0, g], recv_sem=q_sem.at[1, g], device_id=mate, device_id_type=MESH,
        )

    def x1_cols(of, b):
        return pl.ds(pl.multiple_of(of * half + b * blk, blk), blk)

    def x1_copy(of, b):
        return pltpu.make_async_remote_copy(
            src_ref=x1.at[:, x1_cols(of, b)], dst_ref=x1.at[:, x1_cols(of, b)],
            send_sem=x1_sem.at[0, b], recv_sem=x1_sem.at[1, b], device_id=mate, device_id_type=MESH,
        )

    def kv_copy(hh):
        return pltpu.make_async_remote_copy(
            src_ref=kv1.at[hh], dst_ref=kv1.at[hh],
            send_sem=kv_sem.at[0, hh], recv_sem=kv_sem.at[1, hh], device_id=mate, device_id_type=MESH,
        )

    def pass_copy(to):
        return pltpu.make_async_remote_copy(
            src_ref=out.at[0, 0], dst_ref=xs, send_sem=pass_sem.at[to], recv_sem=pass_sem.at[2],
            device_id={"section": jnp.minimum(s + 1 + to, sections - 1)}, device_id_type=MESH,
        )

    for copy in local:
        copy.wait()

    send_stage(0)
    gain_copy.start()

    @pl.when(side == 0)
    def _():
        for hh in range(1, mine_heads):
            send_stage(hh)
    send_hidden()

    @pl.when(side == 1)
    def _():
        for hh in range(1, mine_heads):
            send_stage(hh)

    @pl.when(side == 0)
    def _():
        for g in range(mine_heads):
            q_copy(g).start()

    def own(k):
        away = k // mine_heads != side

        def got(which):
            pl.when(away)(lambda: w_copy(k, which, 4, f).wait_recv())

        got(tail)
        for way in (2, 3):
            w_start(k, tail, way, f)
        got(main)
        for way in range(5):
            w_start(k, main, way, f)
        for way in (0, 1, 4):
            w_start(k, tail, way, f)

    def rope_queries(ref, first, count):
        def one(h, _):
            cols = pl.ds(pl.multiple_of((first + h) * HD, HD), HD)
            u = ref[:, cols].astype(jnp.float32)
            ref[:, cols] = rope(u, cos_ref[...], sin_ref[...]).astype(jnp.bfloat16)
            return 0
        lax.fori_loop(0, count, one, 0)

    pl.when(side == 1)(lambda: own(mine_heads))
    pl.when(side == 0)(lambda: own(0))

    for load in loads:
        load.wait()

    @pl.when(side == 1)
    def _():
        q_local(1).wait()
        rope_queries(q1, 0, width // HD)

    @pl.when(side == 0)
    def _():
        q_local(0).wait()
        rope_queries(q0, 0, half // HD)

    pl.when(side == 1)(lambda: own(0))

    def relay(k, which, origin, ways):
        w_copy(k, which, 4, origin).wait_recv()
        for way in ways:
            w_start(k, which, way, origin)

    def drain(k, which, origin, ways):
        for way in ways:
            on_way(way, lambda way=way: w_copy(k, which, way, origin).wait_send())

    def sides(t, act):
        for sign, way in ((-1, 1), (1, 0)):
            far = o - t if sign < 0 else o + t
            there = (far >= 0) if sign < 0 else ((far < outer) & (t > 0))
            act(far, there, way)

    def around(there, act):
        for d in range(1, inner):
            pl.when(there & (i - d >= 0))(lambda d=d: act(i - d, 3))
            pl.when(there & (i + d < inner))(lambda d=d: act(i + d, 2))

    def along_outer(k, t, receive):
        def act(far, there, way):
            pl.when(there)(lambda: receive(k, main, index(far, i, core), (way, 2, 3, 4)))
        sides(t, act)

        def act_tail(far, there, way):
            pl.when(there)(lambda: receive(k, tail, index(far, i, core), (way, 4)))
            around(there, lambda ii, _: receive(k, tail, index(far, ii, core), (way, 4)))
        sides(t, act_tail)

    def along_inner(k, t, receive):
        def act(far, there, _):
            around(there, lambda ii, way: receive(k, main, index(far, ii, core), (way, 4)))
        sides(t, act)

    def first_inner(k, receive):
        around(o >= 0, lambda ii, way: receive(k, tail, index(o, ii, core), (way, 0, 1, 4)))

    def other_core(k):
        def one(c, _):
            for which in (main, tail):
                w_copy(k, which, 4, 2 * c + 1 - core).wait_recv()
            return 0
        lax.fori_loop(0, chips, one, 0)

    row = lax.broadcasted_iota(jnp.int32, (rows, rows), 0)
    col = lax.broadcasted_iota(jnp.int32, (rows, rows), 1)
    scale = math.log2(math.e) / math.sqrt(HD)

    def scaled(src, cols, layer):
        x = src[:, cols].astype(jnp.float32)
        xg[:, cols] = (x * gains[layer, :, cols]).astype(jnp.bfloat16)
        square = x * x
        total = square[:, :HD]
        for at in range(1, square.shape[1] // HD):
            total += square[:, at * HD:(at + 1) * HD]
        ssq[layer] += total

    def project(k, first, count, fresh):
        cols = pl.ds(pl.multiple_of(first * blk, blk), count * blk)
        b = w[k, pl.ds(first * 2, count * 2)].reshape(count * blk, 2 * HD)
        y = jnp.dot(xg[:, cols], b, preferred_element_type=jnp.float32)
        acc[k] = y if fresh else acc[k] + y

    def row_scale(layer):
        return lax.rsqrt(jnp.sum(ssq[layer], axis=-1, keepdims=True) / width + EPS)

    def finish(k, r, ref, at):
        y = acc[k] * r
        ref[at, 0] = rope(y[:, :HD], cos_ref[...], sin_ref[...]).astype(jnp.bfloat16)
        ref[at, 1] = y[:, HD:].astype(jnp.bfloat16)

    def attend(q_ref, q_first, k, v, x_ref, x_first, write):
        v = jnp.concatenate([v, jnp.ones((rows, HD), jnp.bfloat16)], axis=1)
        allowed = (col <= row)[None]
        q = jnp.concatenate(
            [q_ref[:, pl.ds(pl.multiple_of(q_first + h * HD, HD), HD)] for h in range(group)], axis=0)
        scores = lax.dot_general(q, k, (((1,), (1,)), ((), ())), preferred_element_type=jnp.float32)
        scores = jnp.where(allowed, scores.reshape(group, rows, rows), -1e30)
        top = jnp.max(scores, axis=-1, keepdims=True)
        p = jnp.exp2((scores - top) * scale).astype(jnp.bfloat16).reshape(group * rows, rows)
        mixed = jnp.dot(p, v, preferred_element_type=jnp.float32)
        mixed = mixed[:, :HD] / mixed[:, HD:]
        for h in range(group):
            cols = pl.ds(pl.multiple_of(x_first + h * HD, HD), HD)
            write(cols, (
                x_ref[:, cols].astype(jnp.float32) + mixed[h * rows:(h + 1) * rows]
            ).astype(jnp.bfloat16))

    def write_x1(cols, value):
        x1[:, cols] = value

    def write_out(cols, value):
        out[0, 0, :, cols] = value

    ssq[...] = jnp.zeros_like(ssq)

    def first_inputs():
        @pl.when(pair == 0)
        def _():
            hid_local.wait()
            for j in range(sections):
                @pl.when(s != j)
                def _(j=j):
                    pltpu.make_async_remote_copy(
                        src_ref=hid.at[0], dst_ref=xs.at[pl.ds(j * part, part)],
                        send_sem=hid_send.at[0], recv_sem=hid_recv.at[j],
                        device_id={"section": 0}, device_id_type=MESH,
                    ).wait_recv()
        if sections > 2:
            pl.when(pair > 0)(lambda: pass_copy(0).wait_recv())
        gain_back.wait_recv()

        def one(b, _):
            scaled(xs, pl.ds(pl.multiple_of(b * blk, blk), blk), 0)
            return 0
        lax.fori_loop(0, chips, one, 0)

    def first_layer(hh):
        other_core(hh)
        project(hh, 0, chips, True)
        finish(hh, row_scale(0), kv0, hh)

    def first_attention(g):
        @pl.when(side == 1)
        def _():
            pltpu.make_async_remote_copy(
                src_ref=q_in.at[0, 0, :, pl.ds(half, gw)], dst_ref=q0.at[:, pl.ds(pl.multiple_of(g * gw, gw), gw)],
                send_sem=q_sem.at[0, g], recv_sem=q_sem.at[1, g], device_id=mate, device_id_type=MESH,
            ).wait_recv()
            rope_queries(q0, g * group, group)
        attend(q0, g * gw, kv0[g, 0], kv0[g, 1], xs, side * half + g * gw, write_x1)
        for b in range(gw // blk):
            x1_copy(side, g * (gw // blk) + b).start()
        def one(b, _):
            scaled(x1, x1_cols(side, g * (gw // blk) + b), 1)
            return 0
        lax.fori_loop(0, gw // blk, one, 0)

    def at(k, t):
        return k * outer + min(t, outer - 1)

    steps = slots * outer
    later = jnp.where(pair > 0, steps, 0) if sections > 2 else 0

    def step(u, _):
        k = u // outer
        t = lax.rem(u, outer)

        @pl.when(u < steps)
        def _():
            @pl.when(t == 0)
            def _():
                pl.when((k + 1 < slots) & ((side == 0) | (k + 1 != mine_heads)))(lambda: own(k + 1))
                first_inner(k, relay)
            along_outer(k, t + 1, relay)
            along_inner(k, t, relay)

        v = u - later

        @pl.when(v == at(mine_heads - 1, 2))
        def _():
            first_inputs()

        for hh in range(mine_heads):
            pl.when(v == at(mine_heads - 1, 2 if hh < mine_heads - 1 else 3))(lambda hh=hh: first_layer(hh))

        spots = [at(mine_heads, 0), at(mine_heads, 2)] + [at(mine_heads, 3)] * (mine_heads - 2)
        for g, spot in enumerate(spots):
            pl.when(v == spot)(lambda g=g: first_attention(g))

        @pl.when(v == at(slots - 1, 2))
        def _():
            for k1 in range(mine_heads, slots - 1):
                other_core(k1)
                project(k1, side * pieces, pieces, True)
        return 0

    lax.fori_loop(0, steps + later, step, 0)

    other_core(slots - 1)
    project(slots - 1, side * pieces, pieces, True)

    def arrive(b, _):
        x1_copy(1 - side, b).wait_recv()
        cols = x1_cols(1 - side, b)
        scaled(x1, cols, 1)
        return 0
    lax.fori_loop(0, pieces, arrive, 0)

    r1 = row_scale(1)
    for hh in range(mine_heads):
        k1 = mine_heads + hh
        project(k1, (1 - side) * pieces, pieces, False)
        finish(k1, r1, kv1, side * mine_heads + hh)
        pl.when(side == 0)(lambda hh=hh: kv_copy(hh).start())

    @pl.when(side == 0)
    def _():
        out[0, 0] = x1[...]

    @pl.when(side == 1)
    def _():
        def one(g, _):
            head = jnp.where(g < mine_heads, mine_heads + g, g - mine_heads)
            pl.when(g >= mine_heads)(lambda: kv_copy(g - mine_heads).wait_recv())
            attend(q1, head * gw, kv1[head, 0], kv1[head, 1], x1, head * gw, write_out)
            return 0
        lax.fori_loop(0, kv_heads, one, 0)
        if sections > 2:
            @pl.when(s < sections - 1)
            def _():
                for to in range(2):
                    pass_copy(to).start()

    for hh in range(mine_heads):
        for which in (tail, main):
            stage_copy(side, hh, which).wait_send()
    gain_copy.wait_send()
    for to in range(2):
        pl.when(s != to)(lambda to=to: hid_copy(to).wait_send())
    if sections > 2:
        @pl.when(pair > 0)
        def _():
            pass
    for b in range(pieces):
        x1_copy(side, b).wait_send()

    @pl.when(side == 0)
    def _():
        for g in range(mine_heads):
            q_copy(g).wait_send()
        for hh in range(mine_heads):
            kv_copy(hh).wait_send()

    if sections > 2:
        @pl.when((side == 1) & (s < sections - 1))
        def _():
            for to in range(2):
                pass_copy(to).wait_send()

    def drain_step(u, _):
        k = u // outer
        t = lax.rem(u, outer)

        @pl.when(t == 0)
        def _():
            for which in (main, tail):
                drain(k, which, f, range(5))
            first_inner(k, drain)
        along_outer(k, t + 1, drain)
        along_inner(k, t, drain)
        return 0

    lax.fori_loop(0, steps, drain_step, 0)


def solution(mesh):
    sections, n = mesh.shape["section"], mesh.shape["fsdp"]
    chips = n // 2
    outer = 4 if chips % 4 == 0 else 1
    inner = chips // outer

    def body(hidden_in, queries, key_weight, value_weight, norm_gain):
        rows, width = queries.shape[2:]
        depth, kvw = key_weight.shape[1:]
        cosine, sine = rope_tables(rows)
        hbm = pl.BlockSpec(memory_space=pltpu.HBM)
        vmem = pl.BlockSpec(memory_space=pltpu.VMEM)
        dma = pltpu.SemaphoreType.DMA
        bf16, f32 = jnp.bfloat16, jnp.float32
        heads = kvw // HD // 2
        return pl.pallas_call(
            functools.partial(kernel, n, sections, outer, inner),
            out_shape=jax.ShapeDtypeStruct(queries.shape, bf16),
            in_specs=[hbm] * 7,
            out_specs=vmem,
            scratch_shapes=[
                pltpu.VMEM((2 * heads, n, depth, 2 * HD), bf16),
                pltpu.VMEM((heads, depth, 2 * HD), bf16),
                pltpu.VMEM((rows, width), bf16),
                pltpu.VMEM((rows, width), bf16),
                pltpu.VMEM((rows, width), bf16),
                pltpu.VMEM((rows, width // 2), bf16),
                pltpu.VMEM((rows, width), bf16),
                pltpu.VMEM((2 * heads, rows, 2 * HD), f32),
                pltpu.VMEM((heads, 2, rows, HD), bf16),
                pltpu.VMEM((2 * heads, 2, rows, HD), bf16),
                pltpu.VMEM((2, 1, width), f32),
                pltpu.VMEM((2, rows, HD), f32),
                pltpu.VMEM((rows, HD), f32),
                pltpu.VMEM((rows, HD), f32),
                dma((2 * heads, 2, n)), dma((2 * heads, 2, 5, chips)), dma((heads, 2)), dma((4 * heads,)),
                dma((4,)), dma((2,)), dma((sections,)), dma((2,)), dma,
                dma((2, heads)), dma((2, chips // 2)), dma((2, heads)), dma((3,)),
            ],
            compiler_params=pltpu.CompilerParams(
                collective_id=0, has_side_effects=True, vmem_limit_bytes=28 * 2**20
            ),
        )(*(
            pltpu.with_memory_space_constraint(x, pltpu.HBM)
            for x in (hidden_in, queries, key_weight, value_weight, norm_gain, jnp.asarray(cosine), jnp.asarray(sine))
        ))

    placed = (
        P("fsdp", "section", None),
        P("section", "fsdp", None, None),
        P("section", "fsdp", None),
        P("section", "fsdp", None),
        P("section", None),
    )
    return jax.shard_map(
        body, mesh=mesh, in_specs=placed, out_specs=P("section", "fsdp", None, None), check_vma=False
    )
```

time: 65.1 us -> 78.7 us (1.21)
  Pallas kernels: 63.9 us -> 77.3 us
    pallas_call x1, Pallas kernels: 63.9 us -> 77.3 us  [body(): pl.pallas_call(functools.partial(kernel, n, sections, outer, inner), out_...]
where the time goes in v1:
time: 78.7 us; the launch traced here: 78.2 us
  Pallas kernels  77.3 us (98%)
  local copies, waits for them, and re-layouts  0.97 us (1%)
    pallas_call x1, Pallas kernels, body(): pl.pallas_call(functools.partial(kernel, n, sections, outer, inner), out_...  77.3 us

profile of v1, /device:TPU:3, one launch (start us, length us, event | category | flops | bytes accessed | tf_op | source)
XLA Modules:
  0.0 78.2 jit_solution(8373582550767257311)
XLA Ops:
  0.0 77.3 %shard_map.73 = bf16[1,1,128,4096]{3,2,1,0:T(8,128)(2,1)S(1)} custom-call(bf16[1,64,4096]{2,1,0:T(8,128)(2,1)} %hid.1, bf16[1,1,128,4096]{3,2,1,0:T(8,128)(2,1)} %q_in.1, bf16[1,256,512]{2,1,0:T(8,128)(2,1)} %kw.1, bf16[1,256,512]{2,1,0:T(8,128)(2,1)} %vw.1, f32[1,4096]{1,0:T(1,128)} %gain_in.1, f32[128,128]{1,0:T(8,128)} %constant.4.clone.cos_in, ...), custom_call_target="tpu_custom_call" | custom-call | tf_op jit(solution)/shard_map/pallas_call | solution.py:541
  77.3 1.0 %copy.9 = bf16[1,1,128,4096]{3,2,1,0:T(8,128)(2,1)} copy(bf16[1,1,128,4096]{3,2,1,0:T(8,128)(2,1)S(1)} %shard_map.73) | data formatting | bytes 2097152

commit v2 on v0

--- a/solution.py
+++ b/solution.py
@@ -29,7 +29,7 @@
     return u * cosine + pltpu.roll(u, HD // 2, 1) * sine
 
 
-def kernel(
+def chain_kernel(
     n, sections, outer, inner,
     hid, q_in, kw, vw, gain_in, cos_in, sin_in,
     out,
@@ -363,6 +363,453 @@
             pl.when(s > 0)(lambda: x_copy.wait_send())
 
 
+ORDER = (
+    "OU00", "OT00", "OM000", "OM110", "OM001", "*Q", "OM010", "OM011", "ZM000", "OT01", "ZM001", "OU01",
+    "Y001", "F00", "ZM010", "Y000", "OT10", "ZM011", "ZM020", "Y010", "ZT00", "ZM021", "Y030", "ZT01", "Y011",
+    "OT11", "OM100", "*X", "Y021", "Y020", "ZM100", "Y031", "ZT02", "*P", "OU10", "*A0", "ZM110", "OU11",
+    "F10", "*A1", "ZM120", "ZT10", "Y110", "ZT11", "*D", "Y100", "*M", "Y120", "Y130", "ZT12", "*H",
+)
+
+
+def pair_kernel(
+    n, outer, inner,
+    hid, q_in, kw, vw, gain_in, cos_in, sin_in,
+    out,
+    w, stage, xs, x1, xb, xr, q0, q1, acc, give, take, kv0, kv1, gains, ssq, cos_ref, sin_ref,
+    w_recv, w_send, stage_send, own_sem, load_sem, gain_sem, hid_sem, hid_own,
+    q_sem, x1_sem, kv_sem, swap0_sem, swap_sem, part_sem,
+):
+    side = lax.axis_index("section")
+    f = lax.axis_index("fsdp")
+    mate = {"section": 1 - side}
+    core = lax.rem(f, 2)
+    chip = f // 2
+    i = lax.rem(chip, inner)
+    o = chip // inner
+    twin = {"fsdp": 2 * chip + 1 - core}
+    rows, width = xs.shape
+    part = hid.shape[1]
+    kvw = kw.shape[2]
+    kv_heads = kvw // HD
+    heads = kv_heads // 2
+    group = width // kvw
+    gw = group * HD
+    depth = kw.shape[1]
+    chips = n // 2
+    blk = width // chips
+    half = width // 2
+    pieces = half // blk
+    per_group = gw // blk
+
+    local = []
+    for hh in range(heads):
+        for to_mate in (False, True):
+            head = (1 - side if to_mate else side) * heads + hh
+            cols = pl.ds(pl.multiple_of(head * HD, HD), HD)
+            at = pl.ds(hh * depth, depth)
+            for kind, src in enumerate((kw, vw)):
+                lanes = pl.ds(kind * HD, HD)
+                dst = stage.at[at, lanes] if to_mate else w.at[side, chip, at, lanes]
+                local.append(pltpu.make_async_copy(src.at[0, :, cols], dst, own_sem.at[len(local)]))
+    for copy in local:
+        copy.start()
+    loads = [
+        pltpu.make_async_copy(src, dst, load_sem.at[at])
+        for at, (src, dst) in enumerate(
+            ((gain_in, gains.at[side]), (cos_in, cos_ref), (sin_in, sin_ref)))
+    ]
+    for load in loads:
+        load.start()
+
+    def q_local(which):
+        if which == 0:
+            return pltpu.make_async_copy(q_in.at[0, 0, :, pl.ds(0, half)], q0, load_sem.at[3])
+        return pltpu.make_async_copy(q_in.at[0, 0], q1, load_sem.at[3])
+
+    for which in range(2):
+        pl.when(side == which)(lambda which=which: q_local(which).start())
+
+    def index(oo, ii):
+        return (oo * inner + ii) * 2 + core
+
+    targets = (
+        (o > 0, index(o - 1, i)),
+        (o < outer - 1, index(o + 1, i)),
+        (i > 0, index(o, i - 1)),
+        (i < inner - 1, index(o, i + 1)),
+    )
+
+    barrier = pltpu.get_barrier_semaphore()
+    for cond, target in targets:
+        pl.when(cond)(lambda target=target: pl.semaphore_signal(
+            barrier, inc=1, device_id={"fsdp": target}, device_id_type=MESH))
+    for device in (twin, mate):
+        pl.semaphore_signal(barrier, inc=1, device_id=device, device_id_type=MESH)
+    expected = (
+        jnp.where(o > 0, 1, 0) + jnp.where(o < outer - 1, 1, 0)
+        + jnp.where(i > 0, 1, 0) + jnp.where(i < inner - 1, 1, 0) + 2
+    )
+    pl.semaphore_wait(barrier, expected)
+
+    deep = heads * depth
+    few = max(16, (deep * 96 // 512 + 8) // 16 * 16)
+    splits = (2, 1)
+    cuts = []
+    for layer in range(2):
+        edges = [(deep - few) * at // splits[layer] // 16 * 16 for at in range(splits[layer])] + [deep - few, deep]
+        cuts.append([pl.ds(a, b - a) for a, b in zip(edges, edges[1:])])
+
+    def w_copy(layer, which, way, origin):
+        piece = w.at[layer, origin, cuts[layer][which]]
+        return pltpu.make_async_remote_copy(
+            src_ref=piece, dst_ref=piece,
+            send_sem=w_send.at[layer, which, way, origin], recv_sem=w_recv.at[layer, which, origin],
+            device_id={"fsdp": targets[way][1]}, device_id_type=MESH,
+        )
+
+    def w_start(layer, which, way, origin):
+        pl.when(targets[way][0])(lambda: w_copy(layer, which, way, origin).start())
+
+    def stage_copy(layer, which):
+        return pltpu.make_async_remote_copy(
+            src_ref=stage.at[cuts[layer][which]], dst_ref=w.at[layer, chip, cuts[layer][which]],
+            send_sem=stage_send.at[which], recv_sem=w_recv.at[layer, which, chip],
+            device_id=mate, device_id_type=MESH,
+        )
+
+    def gain_copy(layer):
+        return pltpu.make_async_remote_copy(
+            src_ref=gain_in, dst_ref=gains.at[layer], send_sem=gain_sem.at[0], recv_sem=gain_sem.at[1],
+            device_id=mate, device_id_type=MESH,
+        )
+
+    def hid_copy(of):
+        return pltpu.make_async_remote_copy(
+            src_ref=hid.at[0], dst_ref=xs.at[pl.ds(pl.multiple_of(of * part, part), part)],
+            send_sem=hid_sem.at[0], recv_sem=hid_sem.at[1], device_id=mate, device_id_type=MESH,
+        )
+
+    hid_local = pltpu.make_async_copy(
+        hid.at[0], xs.at[pl.ds(pl.multiple_of(side * part, part), part)], hid_own)
+
+    def q_copy(g):
+        return pltpu.make_async_remote_copy(
+            src_ref=q_in.at[0, 0, :, pl.ds(half + g * gw, gw)], dst_ref=q0.at[:, pl.ds(g * gw, gw)],
+            send_sem=q_sem.at[0, g], recv_sem=q_sem.at[1, g], device_id=mate, device_id_type=MESH,
+        )
+
+    def x1_copy(of, b):
+        cols = pl.ds(pl.multiple_of(of * half + b * blk, blk), blk)
+        return pltpu.make_async_remote_copy(
+            src_ref=x1.at[:, cols], dst_ref=x1.at[:, cols],
+            send_sem=x1_sem.at[0, b], recv_sem=x1_sem.at[1, b], device_id=mate, device_id_type=MESH,
+        )
+
+    def kv_copy(hh):
+        return pltpu.make_async_remote_copy(
+            src_ref=kv1.at[hh], dst_ref=kv1.at[hh],
+            send_sem=kv_sem.at[0, hh], recv_sem=kv_sem.at[1, hh], device_id=mate, device_id_type=MESH,
+        )
+
+    swap0 = pltpu.make_async_remote_copy(
+        src_ref=xb.at[0, 1 - core], dst_ref=xr.at[0], send_sem=swap0_sem.at[0], recv_sem=swap0_sem.at[1],
+        device_id=twin, device_id_type=MESH,
+    )
+
+    def swap_copy(c):
+        cols = pl.ds(pl.multiple_of(c * depth, depth), depth)
+        return pltpu.make_async_remote_copy(
+            src_ref=xb.at[1, 1 - core, :, cols], dst_ref=xr.at[1, :, cols],
+            send_sem=swap_sem.at[0, c], recv_sem=swap_sem.at[1, c], device_id=twin, device_id_type=MESH,
+        )
+
+    def part_copy(layer, hh):
+        return pltpu.make_async_remote_copy(
+            src_ref=give.at[layer, hh], dst_ref=take.at[layer, hh],
+            send_sem=part_sem.at[0, layer, hh], recv_sem=part_sem.at[1, layer, hh],
+            device_id=twin, device_id_type=MESH,
+        )
+
+    for copy in local:
+        copy.wait()
+
+    for layer in range(2):
+        @pl.when(side == layer)
+        def _(layer=layer):
+            for which in range(splits[layer] + 1):
+                stage_copy(layer, which).start()
+    gain_copy(side).start()
+    hid_copy(side).start()
+    hid_local.start()
+
+    @pl.when(side == 0)
+    def _():
+        for g in range(heads):
+            q_copy(g).start()
+
+    def rope_queries(ref, first, count):
+        def one(h, _):
+            cols = pl.ds(pl.multiple_of((first + h) * HD, HD), HD)
+            u = ref[:, cols].astype(jnp.float32)
+            ref[:, cols] = rope(u, cos_ref[...], sin_ref[...]).astype(jnp.bfloat16)
+            return 0
+        lax.fori_loop(0, count, one, 0)
+
+    def relay(layer, which, origin, ways):
+        w_copy(layer, which, 0, origin).wait_recv()
+        for way in ways:
+            w_start(layer, which, way, origin)
+
+    def drain(layer, which, origin, ways):
+        for way in ways:
+            pl.when(targets[way][0])(lambda way=way: w_copy(layer, which, way, origin).wait_send())
+
+    def sides(t, act):
+        if t == 0:
+            act(o, None, 0)
+        else:
+            act(o - t, o - t >= 0, 1)
+            act(o + t, o + t < outer, 0)
+
+    def around(there, act):
+        for d in range(1, inner):
+            for cond, ii, way in ((i - d >= 0, i - d, 3), (i + d < inner, i + d, 2)):
+                pl.when(cond if there is None else there & cond)(lambda ii=ii, way=way: act(ii, way))
+
+    def own(kind, layer, on, which, receive):
+        ways = {"OM": (0, 1, 2, 3), "OT": (2, 3), "OU": (0, 1)}[kind]
+
+        @pl.when(side == on)
+        def _():
+            if receive is relay:
+                if on != layer and kind != "OU":
+                    w_copy(layer, which, 0, chip).wait_recv()
+                for way in ways:
+                    w_start(layer, which, way, chip)
+            else:
+                drain(layer, which, chip, ways)
+
+    def far(t, act):
+        sides(t, lambda oo, there, way: pl.when(there)(lambda: act(oo, way)))
+
+    def move(kind, layer, t, which, receive):
+        tail = splits[layer]
+        if kind[0] == "O":
+            own(kind, layer, t, tail if which is None else which, receive)
+        elif kind == "F":
+            around(None, lambda ii, way: receive(layer, tail, o * inner + ii, (way, 0, 1)))
+        elif kind == "ZM":
+            far(t + 1, lambda oo, way: receive(layer, which, oo * inner + i, (way, 2, 3)))
+        elif kind == "ZT":
+            def both(oo, there, way):
+                pl.when(there)(lambda: receive(layer, tail, oo * inner + i, (way,)))
+                around(there, lambda ii, _: receive(layer, tail, oo * inner + ii, (way,)))
+            sides(t + 1, both)
+        elif kind == "Y":
+            sides(t, lambda oo, there, _: around(
+                there, lambda ii, way: receive(layer, which, oo * inner + ii, (way,))))
+
+    row = lax.broadcasted_iota(jnp.int32, (rows, rows), 0)
+    col = lax.broadcasted_iota(jnp.int32, (rows, rows), 1)
+    scale = math.log2(math.e) / math.sqrt(HD)
+
+    def scaled(src, c, layer):
+        cols = pl.ds(pl.multiple_of(c * blk, blk), blk)
+        x = src[:, cols].astype(jnp.float32)
+        y = (x * gains[layer, :, cols]).astype(jnp.bfloat16)
+        for kind in range(2):
+            xb[layer, kind, :, pl.ds(pl.multiple_of(c * depth, depth), depth)] = y[:, kind * depth:(kind + 1) * depth]
+        square = x * x
+        total = square[:, :HD]
+        for at in range(1, blk // HD):
+            total += square[:, at * HD:(at + 1) * HD]
+        ssq[layer] += total
+
+    def project(layer, hh, first, count, fresh):
+        cols = pl.ds(pl.multiple_of(first * depth, depth), count * depth)
+        a = jnp.concatenate([xb[layer, core, :, cols], xr[layer, :, cols]], axis=0)
+        b = w[layer, pl.ds(first, count), hh * depth:(hh + 1) * depth].reshape(count * depth, 2 * HD)
+        y = jnp.dot(a, b, preferred_element_type=jnp.float32)
+        if fresh:
+            acc[layer, hh] = y[:rows]
+            give[layer, hh] = y[rows:]
+        else:
+            acc[layer, hh] += y[:rows]
+            give[layer, hh] += y[rows:]
+
+    def finish(layer, hh, ref, at):
+        part_copy(layer, hh).wait_recv()
+        r = lax.rsqrt(jnp.sum(ssq[layer], axis=-1, keepdims=True) / width + EPS)
+        y = (acc[layer, hh] + take[layer, hh]) * r
+        ref[at, 0] = rope(y[:, :HD], cos_ref[...], sin_ref[...]).astype(jnp.bfloat16)
+        ref[at, 1] = y[:, HD:].astype(jnp.bfloat16)
+
+    def attend(q_ref, q_first, k, v, x_ref, x_first, write):
+        v = jnp.concatenate([v, jnp.ones((rows, HD), jnp.bfloat16)], axis=1)
+        allowed = (col <= row)[None]
+        q = jnp.concatenate(
+            [q_ref[:, pl.ds(pl.multiple_of(q_first + h * HD, HD), HD)] for h in range(group)], axis=0)
+        scores = lax.dot_general(q, k, (((1,), (1,)), ((), ())), preferred_element_type=jnp.float32)
+        scores = jnp.where(allowed, scores.reshape(group, rows, rows), -1e30)
+        top = jnp.max(scores, axis=-1, keepdims=True)
+        p = jnp.exp2((scores - top) * scale).astype(jnp.bfloat16).reshape(group * rows, rows)
+        mixed = jnp.dot(p, v, preferred_element_type=jnp.float32)
+        mixed = mixed[:, :HD] / mixed[:, HD:]
+        for h in range(group):
+            cols = pl.ds(pl.multiple_of(x_first + h * HD, HD), HD)
+            write(cols, (
+                x_ref[:, cols].astype(jnp.float32) + mixed[h * rows:(h + 1) * rows]
+            ).astype(jnp.bfloat16))
+
+    def write_x1(cols, value):
+        x1[:, cols] = value
+
+    def write_out(cols, value):
+        out[0, 0, :, cols] = value
+
+    def queries_in():
+        for load in loads:
+            load.wait()
+
+        @pl.when(side == 1)
+        def _():
+            q_local(1).wait()
+            rope_queries(q1, 0, width // HD)
+
+        @pl.when(side == 0)
+        def _():
+            q_local(0).wait()
+            rope_queries(q0, 0, half // HD)
+        ssq[...] = jnp.zeros_like(ssq)
+
+    def inputs_in():
+        hid_local.wait()
+        hid_copy(1 - side).wait_recv()
+        gain_copy(1 - side).wait_recv()
+
+        def one(c, _):
+            scaled(xs, c, 0)
+            return 0
+        lax.fori_loop(0, chips, one, 0)
+        swap0.start()
+
+    def first_layer():
+        swap0.wait_recv()
+        for hh in range(heads):
+            project(0, hh, 0, chips, True)
+            part_copy(0, hh).start()
+        for hh in range(heads):
+            finish(0, hh, kv0, hh)
+
+    def first_attention(g):
+        @pl.when(side == 1)
+        def _():
+            q_copy(g).wait_recv()
+            rope_queries(q0, g * group, group)
+        attend(q0, g * gw, kv0[g, 0], kv0[g, 1], xs, side * half + g * gw, write_x1)
+
+        def one(b, _):
+            x1_copy(side, b).start()
+            scaled(x1, side * pieces + b, 1)
+            swap_copy(side * pieces + b).start()
+            return 0
+        lax.fori_loop(g * per_group, (g + 1) * per_group, one, 0)
+
+    def own_half():
+        def one(b, _):
+            swap_copy(side * pieces + b).wait_recv()
+            return 0
+        lax.fori_loop(0, pieces, one, 0)
+        for hh in range(heads):
+            project(1, hh, side * pieces, pieces, True)
+
+    def mate_in(b, _):
+        c = (1 - side) * pieces + b
+        x1_copy(1 - side, b).wait_recv()
+        scaled(x1, c, 1)
+        swap_copy(c).start()
+        return 0
+
+    def drain_layer(layer):
+        for kind, at, t, which in moves:
+            if at == layer:
+                move(kind, at, t, which, drain)
+
+    moves = []
+    for word in ORDER:
+        if word[0] == "*":
+            if word == "*Q":
+                queries_in()
+            elif word == "*X":
+                inputs_in()
+            elif word == "*P":
+                first_layer()
+            elif word[1] == "A":
+                first_attention(int(word[2]))
+            elif word == "*D":
+                drain_layer(0)
+            elif word == "*H":
+                own_half()
+            elif word == "*M":
+                lax.fori_loop(0, pieces // 2, mate_in, 0)
+        else:
+            kind = word.rstrip("0123456789")
+            digits = [int(d) for d in word[len(kind):]]
+            step = (kind, digits[0], digits[1], digits[2] if len(digits) > 2 else None)
+            moves.append(step)
+            move(*step, relay)
+
+    lax.fori_loop(pieces // 2, pieces, mate_in, 0)
+
+    def wait_swap(b, _):
+        swap_copy((1 - side) * pieces + b).wait_recv()
+        return 0
+    lax.fori_loop(0, pieces, wait_swap, 0)
+    for hh in range(heads):
+        project(1, hh, (1 - side) * pieces, pieces, False)
+        part_copy(1, hh).start()
+    for hh in range(heads):
+        finish(1, hh, kv1, side * heads + hh)
+        pl.when(side == 0)(lambda hh=hh: kv_copy(hh).start())
+
+    @pl.when(side == 0)
+    def _():
+        out[0, 0] = x1[...]
+
+    @pl.when(side == 1)
+    def _():
+        def one(g, _):
+            head = jnp.where(g < heads, heads + g, g - heads)
+            pl.when(g >= heads)(lambda: kv_copy(g - heads).wait_recv())
+            attend(q1, head * gw, kv1[head, 0], kv1[head, 1], x1, head * gw, write_out)
+            return 0
+        lax.fori_loop(0, kv_heads, one, 0)
+
+    drain_layer(1)
+    for layer in range(2):
+        @pl.when(side == layer)
+        def _(layer=layer):
+            for which in range(splits[layer] + 1):
+                stage_copy(layer, which).wait_send()
+    gain_copy(side).wait_send()
+    hid_copy(side).wait_send()
+    swap0.wait_send()
+    for c in range(chips):
+        swap_copy(c).wait_send()
+    for layer in range(2):
+        for hh in range(heads):
+            part_copy(layer, hh).wait_send()
+    for b in range(pieces):
+        x1_copy(side, b).wait_send()
+
+    @pl.when(side == 0)
+    def _():
+        for g in range(heads):
+            q_copy(g).wait_send()
+        for hh in range(heads):
+            kv_copy(hh).wait_send()
+
+
 def solution(mesh):
     sections, n = mesh.shape["section"], mesh.shape["fsdp"]
     chips = n // 2
@@ -377,12 +824,35 @@
         vmem = pl.BlockSpec(memory_space=pltpu.VMEM)
         dma = pltpu.SemaphoreType.DMA
         bf16, f32 = jnp.bfloat16, jnp.float32
-        return pl.pallas_call(
-            functools.partial(kernel, n, sections, outer, inner),
-            out_shape=jax.ShapeDtypeStruct(queries.shape, bf16),
-            in_specs=[hbm] * 7,
-            out_specs=vmem,
-            scratch_shapes=[
+        if sections == 2 and outer == 4 and depth % HD == 0:
+            heads = kvw // HD // 2
+            pieces = chips // 2
+            run = functools.partial(pair_kernel, n, outer, inner)
+            scratch = [
+                pltpu.VMEM((2, chips, heads * depth, 2 * HD), bf16),
+                pltpu.VMEM((heads * depth, 2 * HD), bf16),
+                pltpu.VMEM((rows, width), bf16),
+                pltpu.VMEM((rows, width), bf16),
+                pltpu.VMEM((2, 2, rows, width // 2), bf16),
+                pltpu.VMEM((2, rows, width // 2), bf16),
+                pltpu.VMEM((rows, width // 2), bf16),
+                pltpu.VMEM((rows, width), bf16),
+                pltpu.VMEM((2, heads, rows, 2 * HD), f32),
+                pltpu.VMEM((2, heads, rows, 2 * HD), f32),
+                pltpu.VMEM((2, heads, rows, 2 * HD), f32),
+                pltpu.VMEM((heads, 2, rows, HD), bf16),
+                pltpu.VMEM((2 * heads, 2, rows, HD), bf16),
+                pltpu.VMEM((2, 1, width), f32),
+                pltpu.VMEM((2, rows, HD), f32),
+                pltpu.VMEM((rows, HD), f32),
+                pltpu.VMEM((rows, HD), f32),
+                dma((2, 3, chips)), dma((2, 3, 4, chips)), dma((3,)), dma((4 * heads,)),
+                dma((4,)), dma((2,)), dma((2,)), dma,
+                dma((2, heads)), dma((2, pieces)), dma((2, heads)), dma((2,)), dma((2, chips)), dma((2, 2, heads)),
+            ]
+        else:
+            run = functools.partial(chain_kernel, n, sections, outer, inner)
+            scratch = [
                 pltpu.VMEM((n, 2, depth, kvw), bf16),
                 pltpu.VMEM((rows, width), bf16),
                 pltpu.VMEM((rows, width), bf16),
@@ -397,7 +867,13 @@
                 pltpu.VMEM((rows, HD), f32),
                 dma((3, n)), dma((3, 5, n)), dma((2,)), dma((sections,)), dma((2,)), dma,
                 dma((2,)), dma((2, kvw // HD)), dma((2,)), dma((4,)),
-            ],
+            ]
+        return pl.pallas_call(
+            run,
+            out_shape=jax.ShapeDtypeStruct(queries.shape, bf16),
+            in_specs=[hbm] * 7,
+            out_specs=vmem,
+            scratch_shapes=scratch,
             compiler_params=pltpu.CompilerParams(
                 collective_id=0, has_side_effects=True, vmem_limit_bytes=28 * 2**20
             ),

time: 65.1 us -> 60.6 us (0.931); the launches traced: 64.9 us -> 59.6 us
  Pallas kernels: 63.9 us -> 58.6 us
    pallas_call x1, Pallas kernels: 63.9 us -> 58.6 us  [body(): pl.pallas_call(run, out_shape=jax.ShapeDtypeStruct(queries.shape, bf16),...]
where the time goes in v2:
time: 60.6 us; the launch traced here: 59.6 us
  Pallas kernels  58.6 us (97%)
  local copies, waits for them, and re-layouts  0.97 us (2%)
    pallas_call x1, Pallas kernels, body(): pl.pallas_call(run, out_shape=jax.ShapeDtypeStruct(queries.shape, bf16),...  58.6 us

profile of v2, /device:TPU:3, one launch (start us, length us, event | category | flops | bytes accessed | tf_op | source)
XLA Modules:
  0.0 59.6 jit_solution(10539353190957639206)
XLA Ops:
  0.0 58.6 %shard_map.73 = bf16[1,1,128,4096]{3,2,1,0:T(8,128)(2,1)S(1)} custom-call(bf16[1,64,4096]{2,1,0:T(8,128)(2,1)} %hid.1, bf16[1,1,128,4096]{3,2,1,0:T(8,128)(2,1)} %q_in.1, bf16[1,256,512]{2,1,0:T(8,128)(2,1)} %kw.1, bf16[1,256,512]{2,1,0:T(8,128)(2,1)} %vw.1, f32[1,4096]{1,0:T(1,128)} %gain_in.1, f32[128,128]{1,0:T(8,128)} %constant.4.clone.cos_in, ...), custom_call_target="tpu_custom_call" | custom-call | tf_op jit(solution)/shard_map/pallas_call | solution.py:871
  58.7 1.0 %copy.9 = bf16[1,1,128,4096]{3,2,1,0:T(8,128)(2,1)} copy(bf16[1,1,128,4096]{3,2,1,0:T(8,128)(2,1)S(1)} %shard_map.73) | data formatting | bytes 2097152

commit v3 on v2

--- a/solution.py
+++ b/solution.py
@@ -364,10 +364,11 @@
 
 
 ORDER = (
-    "OU00", "OT00", "OM000", "OM110", "OM001", "*Q", "OM010", "OM011", "ZM000", "OT01", "ZM001", "OU01",
-    "Y001", "F00", "ZM010", "Y000", "OT10", "ZM011", "ZM020", "Y010", "ZT00", "ZM021", "Y030", "ZT01", "Y011",
-    "OT11", "OM100", "*X", "Y021", "Y020", "ZM100", "Y031", "ZT02", "*P", "OU10", "*A0", "ZM110", "OU11",
-    "F10", "*A1", "ZM120", "ZT10", "Y110", "ZT11", "*D", "Y100", "*M", "Y120", "Y130", "ZT12", "*H",
+    "OT11", "OM000", "OM110", "OT00", "OM001", "OM111", "*Q", "OM010", "OM011", "OT01", "OU01", "ZM000",
+    "ZM001", "F00", "OM101", "OU00", "ZM011", "ZM010", "ZM021", "ZM020", "ZT00", "*X", "Y010", "Y011", "ZT01",
+    "OM100", "Y001", "Y020", "Y031", "OT10", "Y000", "Y021", "*R0", "ZT02", "Y030", "*P", "ZM101", "ZM100",
+    "*A0", "OU11", "ZM110", "ZM111", "OU10", "F10", "*R1", "*A1", "*C", "*D", "ZM120", "Y101", "Y100",
+    "ZM121", "ZT10", "ZT11", "*M", "Y110", "Y120", "Y130", "*S", "Y111", "Y121", "Y131", "*T", "ZT12",
 )
 
 
@@ -453,14 +454,12 @@
 
     deep = heads * depth
     few = max(16, (deep * 96 // 512 + 8) // 16 * 16)
-    splits = (2, 1)
-    cuts = []
-    for layer in range(2):
-        edges = [(deep - few) * at // splits[layer] // 16 * 16 for at in range(splits[layer])] + [deep - few, deep]
-        cuts.append([pl.ds(a, b - a) for a, b in zip(edges, edges[1:])])
+    early = (heads - 1) * depth
+    cuts = (pl.ds(0, early), pl.ds(early, deep - few - early), pl.ds(deep - few, few))
+    tail = 2
 
     def w_copy(layer, which, way, origin):
-        piece = w.at[layer, origin, cuts[layer][which]]
+        piece = w.at[layer, origin, cuts[which]]
         return pltpu.make_async_remote_copy(
             src_ref=piece, dst_ref=piece,
             send_sem=w_send.at[layer, which, way, origin], recv_sem=w_recv.at[layer, which, origin],
@@ -472,7 +471,7 @@
 
     def stage_copy(layer, which):
         return pltpu.make_async_remote_copy(
-            src_ref=stage.at[cuts[layer][which]], dst_ref=w.at[layer, chip, cuts[layer][which]],
+            src_ref=stage.at[cuts[which]], dst_ref=w.at[layer, chip, cuts[which]],
             send_sem=stage_send.at[which], recv_sem=w_recv.at[layer, which, chip],
             device_id=mate, device_id_type=MESH,
         )
@@ -536,7 +535,7 @@
     for layer in range(2):
         @pl.when(side == layer)
         def _(layer=layer):
-            for which in range(splits[layer] + 1):
+            for which in range(3):
                 stage_copy(layer, which).start()
     gain_copy(side).start()
     hid_copy(side).start()
@@ -548,12 +547,16 @@
             q_copy(g).start()
 
     def rope_queries(ref, first, count):
-        def one(h, _):
-            cols = pl.ds(pl.multiple_of((first + h) * HD, HD), HD)
-            u = ref[:, cols].astype(jnp.float32)
-            ref[:, cols] = rope(u, cos_ref[...], sin_ref[...]).astype(jnp.bfloat16)
-            return 0
-        lax.fori_loop(0, count, one, 0)
+        together = math.gcd(count, 4)
+
+        def one(at, _):
+            cosine, sine = cos_ref[...], sin_ref[...]
+            for h in range(together):
+                cols = pl.ds(pl.multiple_of((first + at * together + h) * HD, HD), HD)
+                u = ref[:, cols].astype(jnp.float32)
+                ref[:, cols] = rope(u, cosine, sine).astype(jnp.bfloat16)
+            return 0
+        lax.fori_loop(0, count // together, one, 0)
 
     def relay(layer, which, origin, ways):
         w_copy(layer, which, 0, origin).wait_recv()
@@ -593,7 +596,6 @@
         sides(t, lambda oo, there, way: pl.when(there)(lambda: act(oo, way)))
 
     def move(kind, layer, t, which, receive):
-        tail = splits[layer]
         if kind[0] == "O":
             own(kind, layer, t, tail if which is None else which, receive)
         elif kind == "F":
@@ -698,14 +700,15 @@
         for hh in range(heads):
             project(0, hh, 0, chips, True)
             part_copy(0, hh).start()
-        for hh in range(heads):
-            finish(0, hh, kv0, hh)
-
-    def first_attention(g):
+
+    def queries_arrive(g):
         @pl.when(side == 1)
         def _():
             q_copy(g).wait_recv()
             rope_queries(q0, g * group, group)
+
+    def first_attention(g):
+        finish(0, g, kv0, g)
         attend(q0, g * gw, kv0[g, 0], kv0[g, 1], xs, side * half + g * gw, write_x1)
 
         def one(b, _):
@@ -715,25 +718,64 @@
             return 0
         lax.fori_loop(g * per_group, (g + 1) * per_group, one, 0)
 
-    def own_half():
+    def mate_in():
         def one(b, _):
-            swap_copy(side * pieces + b).wait_recv()
+            c = (1 - side) * pieces + b
+            x1_copy(1 - side, b).wait_recv()
+            scaled(x1, c, 1)
+            swap_copy(c).start()
             return 0
         lax.fori_loop(0, pieces, one, 0)
+
+    def swapped(of):
+        def one(b, _):
+            swap_copy(of * pieces + b).wait_recv()
+            return 0
+        lax.fori_loop(0, pieces, one, 0)
+
+    def second_layer(hh, first, count, fresh, send=True):
+        project(1, hh, first, count, fresh)
+        if send:
+            part_copy(1, hh).start()
+
+    def second_done(hh):
+        finish(1, hh, kv1, side * heads + hh)
+
+    def send_done(hh):
+        @pl.when(side == 0)
+        def _():
+            second_done(hh)
+            kv_copy(hh).start()
+
+    def first_side_in():
+        @pl.when(side == 0)
+        def _():
+            mate_in()
+            out[0, 0] = x1[...]
+            swapped(1)
+        swapped(side)
+
+    def early_heads():
+        for hh in range(heads - 1):
+            pl.when(side == 0)(lambda hh=hh: second_layer(hh, 0, chips, True))
+            pl.when(side == 1)(lambda hh=hh: second_layer(hh, side * pieces, pieces, True, send=False))
+
+    def settle_first():
+        for layer in range(2):
+            @pl.when(side == layer)
+            def _(layer=layer):
+                for which in range(3):
+                    stage_copy(layer, which).wait_send()
+        gain_copy(side).wait_send()
+        hid_copy(side).wait_send()
+        swap0.wait_send()
         for hh in range(heads):
-            project(1, hh, side * pieces, pieces, True)
-
-    def mate_in(b, _):
-        c = (1 - side) * pieces + b
-        x1_copy(1 - side, b).wait_recv()
-        scaled(x1, c, 1)
-        swap_copy(c).start()
-        return 0
-
-    def drain_layer(layer):
-        for kind, at, t, which in moves:
-            if at == layer:
-                move(kind, at, t, which, drain)
+            part_copy(0, hh).wait_send()
+
+    def drain_moves(layers):
+        for step in [step for step in moves if step[1] in layers]:
+            moves.remove(step)
+            move(*step, drain)
 
     moves = []
     for word in ORDER:
@@ -746,12 +788,19 @@
                 first_layer()
             elif word[1] == "A":
                 first_attention(int(word[2]))
+            elif word == "*C":
+                settle_first()
             elif word == "*D":
-                drain_layer(0)
-            elif word == "*H":
-                own_half()
+                drain_moves((0,))
+            elif word[1] == "R":
+                queries_arrive(int(word[2]))
             elif word == "*M":
-                lax.fori_loop(0, pieces // 2, mate_in, 0)
+                first_side_in()
+            elif word == "*S":
+                early_heads()
+            elif word == "*T":
+                for hh in range(heads - 1):
+                    send_done(hh)
         else:
             kind = word.rstrip("0123456789")
             digits = [int(d) for d in word[len(kind):]]
@@ -759,46 +808,31 @@
             moves.append(step)
             move(*step, relay)
 
-    lax.fori_loop(pieces // 2, pieces, mate_in, 0)
-
-    def wait_swap(b, _):
-        swap_copy((1 - side) * pieces + b).wait_recv()
-        return 0
-    lax.fori_loop(0, pieces, wait_swap, 0)
-    for hh in range(heads):
-        project(1, hh, (1 - side) * pieces, pieces, False)
-        part_copy(1, hh).start()
-    for hh in range(heads):
-        finish(1, hh, kv1, side * heads + hh)
-        pl.when(side == 0)(lambda hh=hh: kv_copy(hh).start())
-
-    @pl.when(side == 0)
-    def _():
-        out[0, 0] = x1[...]
-
     @pl.when(side == 1)
     def _():
+        mate_in()
+        swapped(0)
+        for hh in range(heads - 1):
+            second_layer(hh, (1 - side) * pieces, pieces, False)
+    second_layer(heads - 1, 0, chips, True)
+    send_done(heads - 1)
+
+    @pl.when(side == 1)
+    def _():
+        for hh in range(heads - 1):
+            second_done(hh)
+
         def one(g, _):
-            head = jnp.where(g < heads, heads + g, g - heads)
-            pl.when(g >= heads)(lambda: kv_copy(g - heads).wait_recv())
-            attend(q1, head * gw, kv1[head, 0], kv1[head, 1], x1, head * gw, write_out)
-            return 0
-        lax.fori_loop(0, kv_heads, one, 0)
-
-    drain_layer(1)
-    for layer in range(2):
-        @pl.when(side == layer)
-        def _(layer=layer):
-            for which in range(splits[layer] + 1):
-                stage_copy(layer, which).wait_send()
-    gain_copy(side).wait_send()
-    hid_copy(side).wait_send()
-    swap0.wait_send()
+            pl.when(g == heads - 1)(lambda: second_done(heads - 1))
+            attend(q1, (heads + g) * gw, kv1[heads + g, 0], kv1[heads + g, 1], x1, (heads + g) * gw, write_out)
+            return 0
+        lax.fori_loop(0, heads, one, 0)
+
+    drain_moves((0, 1))
     for c in range(chips):
         swap_copy(c).wait_send()
-    for layer in range(2):
-        for hh in range(heads):
-            part_copy(layer, hh).wait_send()
+    for hh in range(heads):
+        part_copy(1, hh).wait_send()
     for b in range(pieces):
         x1_copy(side, b).wait_send()
 
@@ -808,6 +842,14 @@
             q_copy(g).wait_send()
         for hh in range(heads):
             kv_copy(hh).wait_send()
+
+    @pl.when(side == 1)
+    def _():
+        def one(g, _):
+            kv_copy(g).wait_recv()
+            attend(q1, g * gw, kv1[g, 0], kv1[g, 1], x1, g * gw, write_out)
+            return 0
+        lax.fori_loop(0, heads, one, 0)
 
 
 def solution(mesh):

time: 60.6 us -> 58.4 us (0.964); the launches traced: 59.6 us -> 58.2 us
  Pallas kernels: 58.6 us -> 57.2 us
    pallas_call x1, Pallas kernels: 58.6 us -> 57.2 us  [body(): pl.pallas_call(run, out_shape=jax.ShapeDtypeStruct(queries.shape, bf16),...]
where the time goes in v3:
time: 58.4 us; the launch traced here: 58.2 us
  Pallas kernels  57.2 us (98%)
  local copies, waits for them, and re-layouts  0.97 us (2%)
    pallas_call x1, Pallas kernels, body(): pl.pallas_call(run, out_shape=jax.ShapeDtypeStruct(queries.shape, bf16),...  57.2 us

profile of v3, /device:TPU:3, one launch (start us, length us, event | category | flops | bytes accessed | tf_op | source)
XLA Modules:
  0.0 58.2 jit_solution(1972929732872835536)
XLA Ops:
  0.0 57.2 %shard_map.73 = bf16[1,1,128,4096]{3,2,1,0:T(8,128)(2,1)S(1)} custom-call(bf16[1,64,4096]{2,1,0:T(8,128)(2,1)} %hid.1, bf16[1,1,128,4096]{3,2,1,0:T(8,128)(2,1)} %q_in.1, bf16[1,256,512]{2,1,0:T(8,128)(2,1)} %kw.1, bf16[1,256,512]{2,1,0:T(8,128)(2,1)} %vw.1, f32[1,4096]{1,0:T(1,128)} %gain_in.1, f32[128,128]{1,0:T(8,128)} %constant.4.clone.cos_in, ...), custom_call_target="tpu_custom_call" | custom-call | tf_op jit(solution)/shard_map/pallas_call | solution.py:913
  57.2 1.0 %copy.9 = bf16[1,1,128,4096]{3,2,1,0:T(8,128)(2,1)} copy(bf16[1,1,128,4096]{3,2,1,0:T(8,128)(2,1)S(1)} %shard_map.73) | data formatting | bytes 2097152

commit v4 on v3

--- a/solution.py
+++ b/solution.py
@@ -364,11 +364,12 @@
 
 
 ORDER = (
-    "OT11", "OM000", "OM110", "OT00", "OM001", "OM111", "*Q", "OM010", "OM011", "OT01", "OU01", "ZM000",
-    "ZM001", "F00", "OM101", "OU00", "ZM011", "ZM010", "ZM021", "ZM020", "ZT00", "*X", "Y010", "Y011", "ZT01",
-    "OM100", "Y001", "Y020", "Y031", "OT10", "Y000", "Y021", "*R0", "ZT02", "Y030", "*P", "ZM101", "ZM100",
-    "*A0", "OU11", "ZM110", "ZM111", "OU10", "F10", "*R1", "*A1", "*C", "*D", "ZM120", "Y101", "Y100",
-    "ZM121", "ZT10", "ZT11", "*M", "Y110", "Y120", "Y130", "*S", "Y111", "Y121", "Y131", "*T", "ZT12",
+    "OM000", "OM001", "OM110", "OT00", "OU00", "OT11", "OM111", "*Q", "OM010", "OM011", "OT01", "OU01",
+    "ZM000", "ZM001", "F00", "OM101", "ZM011", "ZM010", "ZM021", "ZM020", "ZT00", "*X", "Y010", "Y011",
+    "ZT01", "OM100", "Y020", "*q", "Y001", "Y031", "OT10", "Y000", "Y021", "*R0", "ZT02", "Y030", "*P",
+    "ZM101", "ZM100", "*A0", "OU11", "ZM110", "ZM111", "OU10", "F10", "*R1", "*A1", "*D", "ZM120", "*C",
+    "Y101", "Y100", "ZM121", "ZT10", "ZT11", "*M", "Y110", "Y120", "Y130", "*S", "Y111", "Y121", "Y131", "*N",
+    "*L", "*T", "ZT12",
 )
 
 
@@ -455,11 +456,14 @@
     deep = heads * depth
     few = max(16, (deep * 96 // 512 + 8) // 16 * 16)
     early = (heads - 1) * depth
-    cuts = (pl.ds(0, early), pl.ds(early, deep - few - early), pl.ds(deep - few, few))
+    cuts = [
+        (pl.ds(0, at), pl.ds(at, deep - few - at), pl.ds(deep - few, few))
+        for at in (deep * 160 // 512 // 16 * 16, early)
+    ]
     tail = 2
 
     def w_copy(layer, which, way, origin):
-        piece = w.at[layer, origin, cuts[which]]
+        piece = w.at[layer, origin, cuts[layer][which]]
         return pltpu.make_async_remote_copy(
             src_ref=piece, dst_ref=piece,
             send_sem=w_send.at[layer, which, way, origin], recv_sem=w_recv.at[layer, which, origin],
@@ -471,7 +475,7 @@
 
     def stage_copy(layer, which):
         return pltpu.make_async_remote_copy(
-            src_ref=stage.at[cuts[which]], dst_ref=w.at[layer, chip, cuts[which]],
+            src_ref=stage.at[cuts[layer][which]], dst_ref=w.at[layer, chip, cuts[layer][which]],
             send_sem=stage_send.at[which], recv_sem=w_recv.at[layer, which, chip],
             device_id=mate, device_id_type=MESH,
         )
@@ -504,10 +508,10 @@
             send_sem=x1_sem.at[0, b], recv_sem=x1_sem.at[1, b], device_id=mate, device_id_type=MESH,
         )
 
-    def kv_copy(hh):
-        return pltpu.make_async_remote_copy(
-            src_ref=kv1.at[hh], dst_ref=kv1.at[hh],
-            send_sem=kv_sem.at[0, hh], recv_sem=kv_sem.at[1, hh], device_id=mate, device_id_type=MESH,
+    def kv_copy(hh, kind):
+        return pltpu.make_async_remote_copy(
+            src_ref=kv1.at[hh, kind], dst_ref=kv1.at[hh, kind],
+            send_sem=kv_sem.at[0, hh, kind], recv_sem=kv_sem.at[1, hh, kind], device_id=mate, device_id_type=MESH,
         )
 
     swap0 = pltpu.make_async_remote_copy(
@@ -639,29 +643,42 @@
             acc[layer, hh] += y[:rows]
             give[layer, hh] += y[rows:]
 
-    def finish(layer, hh, ref, at):
+    def finish(layer, hh, ref, at, then=None):
         part_copy(layer, hh).wait_recv()
         r = lax.rsqrt(jnp.sum(ssq[layer], axis=-1, keepdims=True) / width + EPS)
         y = (acc[layer, hh] + take[layer, hh]) * r
         ref[at, 0] = rope(y[:, :HD], cos_ref[...], sin_ref[...]).astype(jnp.bfloat16)
+        if then is not None:
+            then(0)
         ref[at, 1] = y[:, HD:].astype(jnp.bfloat16)
-
-    def attend(q_ref, q_first, k, v, x_ref, x_first, write):
-        v = jnp.concatenate([v, jnp.ones((rows, HD), jnp.bfloat16)], axis=1)
+        if then is not None:
+            then(1)
+
+    def attend(q_ref, q_first, kv_ref, head, x_ref, x_first, write, ready=None):
+        if ready is not None:
+            ready(0)
+        k = kv_ref[head, 0]
         allowed = (col <= row)[None]
-        q = jnp.concatenate(
-            [q_ref[:, pl.ds(pl.multiple_of(q_first + h * HD, HD), HD)] for h in range(group)], axis=0)
-        scores = lax.dot_general(q, k, (((1,), (1,)), ((), ())), preferred_element_type=jnp.float32)
-        scores = jnp.where(allowed, scores.reshape(group, rows, rows), -1e30)
-        top = jnp.max(scores, axis=-1, keepdims=True)
-        p = jnp.exp2((scores - top) * scale).astype(jnp.bfloat16).reshape(group * rows, rows)
-        mixed = jnp.dot(p, v, preferred_element_type=jnp.float32)
-        mixed = mixed[:, :HD] / mixed[:, HD:]
-        for h in range(group):
-            cols = pl.ds(pl.multiple_of(x_first + h * HD, HD), HD)
-            write(cols, (
-                x_ref[:, cols].astype(jnp.float32) + mixed[h * rows:(h + 1) * rows]
-            ).astype(jnp.bfloat16))
+        batch = group // 4
+        probs = []
+        for first in range(0, group, batch):
+            q = jnp.concatenate(
+                [q_ref[:, pl.ds(pl.multiple_of(q_first + (first + h) * HD, HD), HD)] for h in range(batch)], axis=0)
+            scores = lax.dot_general(q, k, (((1,), (1,)), ((), ())), preferred_element_type=jnp.float32)
+            scores = jnp.where(allowed, scores.reshape(batch, rows, rows), -1e30)
+            top = jnp.max(scores, axis=-1, keepdims=True)
+            probs.append(jnp.exp2((scores - top) * scale).astype(jnp.bfloat16).reshape(batch * rows, rows))
+        if ready is not None:
+            ready(1)
+        v = jnp.concatenate([kv_ref[head, 1], jnp.ones((rows, HD), jnp.bfloat16)], axis=1)
+        for first, p in zip(range(0, group, batch), probs):
+            mixed = jnp.dot(p, v, preferred_element_type=jnp.float32)
+            mixed = mixed[:, :HD] / mixed[:, HD:]
+            for h in range(batch):
+                cols = pl.ds(pl.multiple_of(x_first + (first + h) * HD, HD), HD)
+                write(cols, (
+                    x_ref[:, cols].astype(jnp.float32) + mixed[h * rows:(h + 1) * rows]
+                ).astype(jnp.bfloat16))
 
     def write_x1(cols, value):
         x1[:, cols] = value
@@ -678,11 +695,13 @@
             q_local(1).wait()
             rope_queries(q1, 0, width // HD)
 
+        ssq[...] = jnp.zeros_like(ssq)
+
+    def queries_mine():
         @pl.when(side == 0)
         def _():
             q_local(0).wait()
             rope_queries(q0, 0, half // HD)
-        ssq[...] = jnp.zeros_like(ssq)
 
     def inputs_in():
         hid_local.wait()
@@ -709,7 +728,7 @@
 
     def first_attention(g):
         finish(0, g, kv0, g)
-        attend(q0, g * gw, kv0[g, 0], kv0[g, 1], xs, side * half + g * gw, write_x1)
+        attend(q0, g * gw, kv0, g, xs, side * half + g * gw, write_x1)
 
         def one(b, _):
             x1_copy(side, b).start()
@@ -738,14 +757,13 @@
         if send:
             part_copy(1, hh).start()
 
-    def second_done(hh):
-        finish(1, hh, kv1, side * heads + hh)
+    def second_done(hh, then=None):
+        finish(1, hh, kv1, side * heads + hh, then)
 
     def send_done(hh):
         @pl.when(side == 0)
         def _():
-            second_done(hh)
-            kv_copy(hh).start()
+            second_done(hh, lambda kind: kv_copy(hh, kind).start())
 
     def first_side_in():
         @pl.when(side == 0)
@@ -754,6 +772,12 @@
             out[0, 0] = x1[...]
             swapped(1)
         swapped(side)
+
+    def second_side_in():
+        @pl.when(side == 1)
+        def _():
+            mate_in()
+            swapped(0)
 
     def early_heads():
         for hh in range(heads - 1):
@@ -782,12 +806,20 @@
         if word[0] == "*":
             if word == "*Q":
                 queries_in()
+            elif word == "*q":
+                queries_mine()
             elif word == "*X":
                 inputs_in()
             elif word == "*P":
                 first_layer()
             elif word[1] == "A":
                 first_attention(int(word[2]))
+            elif word[1] in "ab":
+                pl.when(side == "ba".index(word[1]))(lambda g=int(word[2]): first_attention(g))
+            elif word == "*L":
+                second_layer(heads - 1, jnp.where(o < outer // 2, 0, inner), chips - inner, True, send=False)
+            elif word == "*N":
+                second_side_in()
             elif word == "*C":
                 settle_first()
             elif word == "*D":
@@ -810,11 +842,9 @@
 
     @pl.when(side == 1)
     def _():
-        mate_in()
-        swapped(0)
         for hh in range(heads - 1):
             second_layer(hh, (1 - side) * pieces, pieces, False)
-    second_layer(heads - 1, 0, chips, True)
+    second_layer(heads - 1, jnp.where(o < outer // 2, (outer - 1) * inner, 0), inner, False)
     send_done(heads - 1)
 
     @pl.when(side == 1)
@@ -824,7 +854,7 @@
 
         def one(g, _):
             pl.when(g == heads - 1)(lambda: second_done(heads - 1))
-            attend(q1, (heads + g) * gw, kv1[heads + g, 0], kv1[heads + g, 1], x1, (heads + g) * gw, write_out)
+            attend(q1, (heads + g) * gw, kv1, heads + g, x1, (heads + g) * gw, write_out)
             return 0
         lax.fori_loop(0, heads, one, 0)
 
@@ -841,13 +871,13 @@
         for g in range(heads):
             q_copy(g).wait_send()
         for hh in range(heads):
-            kv_copy(hh).wait_send()
+            for kind in range(2):
+                kv_copy(hh, kind).wait_send()
 
     @pl.when(side == 1)
     def _():
         def one(g, _):
-            kv_copy(g).wait_recv()
-            attend(q1, g * gw, kv1[g, 0], kv1[g, 1], x1, g * gw, write_out)
+            attend(q1, g * gw, kv1, g, x1, g * gw, write_out, lambda kind: kv_copy(g, kind).wait_recv())
             return 0
         lax.fori_loop(0, heads, one, 0)
 
@@ -890,7 +920,7 @@
                 pltpu.VMEM((rows, HD), f32),
                 dma((2, 3, chips)), dma((2, 3, 4, chips)), dma((3,)), dma((4 * heads,)),
                 dma((4,)), dma((2,)), dma((2,)), dma,
-                dma((2, heads)), dma((2, pieces)), dma((2, heads)), dma((2,)), dma((2, chips)), dma((2, 2, heads)),
+                dma((2, heads)), dma((2, pieces)), dma((2, heads, 2)), dma((2,)), dma((2, chips)), dma((2, 2, heads)),
             ]
         else:
             run = functools.partial(chain_kernel, n, sections, outer, inner)

time: 58.4 us -> 58.1 us (level)
  Pallas kernels: 57.2 us -> 56.5 us
    pallas_call x1, Pallas kernels: 57.2 us -> 56.5 us  [body(): pl.pallas_call(run, out_shape=jax.ShapeDtypeStruct(queries.shape, bf16),...]
where the time goes in v4:
time: 58.1 us; the launch traced here: 57.5 us
  Pallas kernels  56.5 us (97%)
  local copies, waits for them, and re-layouts  0.97 us (2%)
    pallas_call x1, Pallas kernels, body(): pl.pallas_call(run, out_shape=jax.ShapeDtypeStruct(queries.shape, bf16),...  56.5 us

profile of v4, /device:TPU:3, one launch (start us, length us, event | category | flops | bytes accessed | tf_op | source)
XLA Modules:
  0.0 57.5 jit_solution(15217095876082833092)
XLA Ops:
  0.0 56.5 %shard_map.73 = bf16[1,1,128,4096]{3,2,1,0:T(8,128)(2,1)S(1)} custom-call(bf16[1,64,4096]{2,1,0:T(8,128)(2,1)} %hid.1, bf16[1,1,128,4096]{3,2,1,0:T(8,128)(2,1)} %q_in.1, bf16[1,256,512]{2,1,0:T(8,128)(2,1)} %kw.1, bf16[1,256,512]{2,1,0:T(8,128)(2,1)} %vw.1, f32[1,4096]{1,0:T(1,128)} %gain_in.1, f32[128,128]{1,0:T(8,128)} %constant.4.clone.cos_in, ...), custom_call_target="tpu_custom_call" | custom-call | tf_op jit(solution)/shard_map/pallas_call | solution.py:943
  56.5 1.0 %copy.9 = bf16[1,1,128,4096]{3,2,1,0:T(8,128)(2,1)} copy(bf16[1,1,128,4096]{3,2,1,0:T(8,128)(2,1)S(1)} %shard_map.73) | data formatting | bytes 2097152

commit v5 on v4

--- a/solution.py
+++ b/solution.py
@@ -541,8 +541,8 @@
         def _(layer=layer):
             for which in range(3):
                 stage_copy(layer, which).start()
+    hid_copy(side).start()
     gain_copy(side).start()
-    hid_copy(side).start()
     hid_local.start()
 
     @pl.when(side == 0)

time: 58.1 us -> 58.1 us (level)
  no operation moved by 1% of the time
where the time goes in v5:
time: 58.1 us; the launch traced here: 57.5 us
  Pallas kernels  56.5 us (97%)
  local copies, waits for them, and re-layouts  0.97 us (2%)
    pallas_call x1, Pallas kernels, body(): pl.pallas_call(run, out_shape=jax.ShapeDtypeStruct(queries.shape, bf16),...  56.5 us

profile of v5, /device:TPU:3, one launch (start us, length us, event | category | flops | bytes accessed | tf_op | source)
XLA Modules:
  0.0 57.5 jit_solution(8637468806476628243)
XLA Ops:
  0.0 56.5 %shard_map.73 = bf16[1,1,128,4096]{3,2,1,0:T(8,128)(2,1)S(1)} custom-call(bf16[1,64,4096]{2,1,0:T(8,128)(2,1)} %hid.1, bf16[1,1,128,4096]{3,2,1,0:T(8,128)(2,1)} %q_in.1, bf16[1,256,512]{2,1,0:T(8,128)(2,1)} %kw.1, bf16[1,256,512]{2,1,0:T(8,128)(2,1)} %vw.1, f32[1,4096]{1,0:T(1,128)} %gain_in.1, f32[128,128]{1,0:T(8,128)} %constant.4.clone.cos_in, ...), custom_call_target="tpu_custom_call" | custom-call | tf_op jit(solution)/shard_map/pallas_call | solution.py:943
  56.5 1.0 %copy.9 = bf16[1,1,128,4096]{3,2,1,0:T(8,128)(2,1)} copy(bf16[1,1,128,4096]{3,2,1,0:T(8,128)(2,1)S(1)} %shard_map.73) | data formatting | bytes 2097152

commit v6 on v5

--- a/solution.py
+++ b/solution.py
@@ -458,7 +458,7 @@
     early = (heads - 1) * depth
     cuts = [
         (pl.ds(0, at), pl.ds(at, deep - few - at), pl.ds(deep - few, few))
-        for at in (deep * 160 // 512 // 16 * 16, early)
+        for at in (deep * 112 // 512 // 16 * 16, early)
     ]
     tail = 2
 

time: 58.1 us -> 58.3 us (level)
  Pallas kernels: 56.5 us -> 57.2 us
    pallas_call x1, Pallas kernels: 56.5 us -> 57.2 us  [body(): pl.pallas_call(run, out_shape=jax.ShapeDtypeStruct(queries.shape, bf16),...]
where the time goes in v6:
time: 58.3 us; the launch traced here: 58.1 us
  Pallas kernels  57.2 us (98%)
  local copies, waits for them, and re-layouts  0.97 us (2%)
    pallas_call x1, Pallas kernels, body(): pl.pallas_call(run, out_shape=jax.ShapeDtypeStruct(queries.shape, bf16),...  57.2 us

profile of v6, /device:TPU:3, one launch (start us, length us, event | category | flops | bytes accessed | tf_op | source)
XLA Modules:
  0.0 58.1 jit_solution(13853264996826613340)
XLA Ops:
  0.0 57.2 %shard_map.73 = bf16[1,1,128,4096]{3,2,1,0:T(8,128)(2,1)S(1)} custom-call(bf16[1,64,4096]{2,1,0:T(8,128)(2,1)} %hid.1, bf16[1,1,128,4096]{3,2,1,0:T(8,128)(2,1)} %q_in.1, bf16[1,256,512]{2,1,0:T(8,128)(2,1)} %kw.1, bf16[1,256,512]{2,1,0:T(8,128)(2,1)} %vw.1, f32[1,4096]{1,0:T(1,128)} %gain_in.1, f32[128,128]{1,0:T(8,128)} %constant.4.clone.cos_in, ...), custom_call_target="tpu_custom_call" | custom-call | tf_op jit(solution)/shard_map/pallas_call | solution.py:943
  57.2 1.0 %copy.9 = bf16[1,1,128,4096]{3,2,1,0:T(8,128)(2,1)} copy(bf16[1,1,128,4096]{3,2,1,0:T(8,128)(2,1)S(1)} %shard_map.73) | data formatting | bytes 2097152
